TPU v7x, 32 devices: a whole 2x2x4 slice. The times are simulated.
32 devices in a mesh: expert: 8 (over z, x), pair: 2 (over core), dp: 2 (over y).
Axes of the slice: x: 2, y: 2, z: 4, core: 2. Of those that a mesh axis runs over, the one named last changes fastest.
Arguments:
- tokens: bfloat16 [128, 196, 768], P(('expert', 'pair', 'dp')), may hold values from -96 to 96
- phi: bfloat16 [768, 16], replicated, may hold values from -0.25 to 0.25
- w_in: bfloat16 [8, 768, 3072], P('expert', None, 'pair'), may hold values from -0.21875 to 0.21875
- w_out: bfloat16 [8, 3072, 768], P('expert', 'pair'), may hold values from -0.109375 to 0.109375
- slot_out: bfloat16 [128, 16, 768], P(('expert', 'pair', 'dp')), may hold values from -6 to 6
- grad_out: bfloat16 [128, 196, 768], P(('expert', 'pair', 'dp')), may hold values from -6 to 6
Outputs:
- token_grad: bfloat16 [128, 196, 768], P(('expert', 'pair', 'dp'))
- phi_grad: float32 [768, 16], replicated
- grad_w_in: bfloat16 [8, 768, 3072], P('expert', 'dp', 'pair')
- grad_w_out: bfloat16 [8, 3072, 768], P('expert', 'pair', 'dp')
All inputs are finite; a program needn't handle non-finite values.
Results may differ from a plain program's by a relative error of at most 0.0086.
Values may be sent and summed in bfloat16 or wider, within the bound.
A program may use at most 128 MiB of HBM per device.

v0:
```python
import jax
import jax.numpy as jnp
from jax import lax
from jax.sharding import PartitionSpec as P


def expert_rows(z_rows, g_rows, w_first, w_second):
    pre = jnp.dot(z_rows, w_first, preferred_element_type=jnp.float32)
    act_full, gelu_back = jax.vjp(jax.nn.gelu, pre)
    act = act_full.astype(jnp.bfloat16)
    dact = lax.dot_general(
        g_rows, w_second, (((1,), (1,)), ((), ())), preferred_element_type=jnp.float32
    )
    dpre = gelu_back(dact)[0].astype(jnp.bfloat16)
    grad_second = lax.dot_general(
        act, g_rows, (((0,), (0,)), ((), ())), preferred_element_type=jnp.float32
    )
    grad_first = lax.dot_general(
        z_rows, dpre, (((0,), (0,)), ((), ())), preferred_element_type=jnp.float32
    )
    back = lax.dot_general(
        dpre, w_first, (((1,), (1,)), ((), ())), preferred_element_type=jnp.float32
    )
    return (grad_first, grad_second, back)


def local(tokens, phi, w_in, w_out, slot_out, grad_out):
    f32 = jnp.float32
    images, _, width = tokens.shape
    groups = lax.axis_size("expert")
    per_group = phi.shape[1] // groups
    experts_here = w_in.shape[0]
    slots = per_group // experts_here
    logits = jnp.einsum("bmd,ds->bms", tokens, phi, preferred_element_type=f32)
    dispatch = jax.nn.softmax(logits, axis=1)
    combine = jax.nn.softmax(logits, axis=2)
    dispatch_low = dispatch.astype(jnp.bfloat16)
    combine_low = combine.astype(jnp.bfloat16)
    slot_in = jnp.einsum("bms,bmd->bsd", dispatch_low, tokens, preferred_element_type=f32).astype(
        jnp.bfloat16
    )
    slot_grad = jnp.einsum(
        "bms,bmd->bsd", combine_low, grad_out, preferred_element_type=f32
    ).astype(jnp.bfloat16)
    outgoing_in = slot_in.reshape(images, groups, per_group, width)
    outgoing_grad = slot_grad.reshape(images, groups, per_group, width)
    arrived_in, arrived_grad = (
        lax.all_to_all(outgoing_in, "expert", split_axis=1, concat_axis=0, tiled=True),
        lax.all_to_all(outgoing_grad, "expert", split_axis=1, concat_axis=0, tiled=True),
    )
    rows_in, rows_grad = (
        lax.all_gather(arrived_in, "pair", axis=0, tiled=True),
        lax.all_gather(arrived_grad, "pair", axis=0, tiled=True),
    )
    count = rows_in.shape[0]
    z_rows = rows_in[:, 0].reshape(count * slots, width)
    g_rows = rows_grad[:, 0].reshape(count * slots, width)
    grad_first, grad_second, back = expert_rows(z_rows, g_rows, w_in[0], w_out[0])
    firsts = [grad_first]
    seconds = [grad_second]
    backs = back.reshape(count, 1, slots, width)
    back_sum = lax.psum_scatter(backs, "pair", scatter_dimension=0, tiled=True)
    grad_w_in = lax.psum_scatter(
        jnp.stack(firsts).astype(jnp.bfloat16), "dp", scatter_dimension=1, tiled=True
    )
    grad_w_out = lax.psum_scatter(
        jnp.stack(seconds).astype(jnp.bfloat16), "dp", scatter_dimension=2, tiled=True
    )
    back_low = back_sum.astype(jnp.bfloat16)
    returned = lax.all_to_all(back_low, "expert", split_axis=0, concat_axis=1, tiled=True)
    slot_in_grad = returned.reshape(images, groups * per_group, width)
    dispatch_grad = jnp.einsum("bmd,bsd->bms", tokens, slot_in_grad, preferred_element_type=f32)
    combine_grad = jnp.einsum("bmd,bsd->bms", grad_out, slot_out, preferred_element_type=f32)
    logit_grad = dispatch * (
        dispatch_grad - jnp.sum(dispatch * dispatch_grad, axis=1, keepdims=True)
    )
    logit_grad = logit_grad + combine * (
        combine_grad - jnp.sum(combine * combine_grad, axis=2, keepdims=True)
    )
    logit_low = logit_grad.astype(jnp.bfloat16)
    token_part = jnp.einsum("bms,bsd->bmd", dispatch_low, slot_in_grad, preferred_element_type=f32)
    token_grad = (
        token_part + jnp.einsum("bms,ds->bmd", logit_low, phi, preferred_element_type=f32)
    ).astype(jnp.bfloat16)
    phi_part = jnp.einsum("bmd,bms->ds", tokens, logit_low, preferred_element_type=f32)
    phi_grad = lax.psum(phi_part, ("expert", "pair", "dp"))
    return (token_grad, phi_grad, grad_w_in, grad_w_out)


def solution(mesh):
    in_specs = (
        P(("expert", "pair", "dp"), None, None),
        P(),
        P("expert", None, "pair"),
        P("expert", "pair", None),
        P(("expert", "pair", "dp"), None, None),
        P(("expert", "pair", "dp"), None, None),
    )
    out_specs = (
        P(("expert", "pair", "dp"), None, None),
        P(),
        P("expert", "dp", "pair"),
        P("expert", "pair", "dp"),
    )
    return jax.shard_map(local, mesh=mesh, in_specs=in_specs, out_specs=out_specs, check_vma=False)
```

profile of v0, /device:TPU:0, one launch (start us, length us, event | category | flops | bytes accessed | tf_op | source)
XLA Modules:
  0.0 153.0 jit_solution(3510893113097627227)
XLA Ops:
  7.2 1.8 %fusion.32 = f32[4,196,16]{1,2,0:T(8,128)S(1)} fusion(bf16[4,196,768]{2,0,1:T(4,128)(2,1)} %param.6, bf16[768,16]{0,1:T(8,128)(2,1)} %param.7), kind=kOutput, calls=%fused_computation.41 | convolution fusion | flops 19267584 | bytes 1278976 | tf_op jit(solution)/shard_map/bmd,ds->bms/dot_general | solution.py:34
  9.0 0.7 fusion.64
  9.7 1.6 %convolution_convert_fusion.3 = bf16[4,16,768]{2,1,0:T(8,128)(2,1)S(1)} fusion(bf16[4,196,768]{2,0,1:T(4,128)(2,1)} %param.11, f32[4,196]{1,0:T(4,128)S(1)} %get-tuple-element.16, f32[4,196,16]{1,2,0:T(8,128)S(1)} %fusion.32), kind=kOutput, calls=%fused_computation.19 | convolution fusion | flops 19355168 | bytes 1355840 | tf_op jit(solution)/shard_map/bms,bmd->bsd/dot_general | solution.py:42
  11.4 0.7 copy.32
  12.1 7.3 %all-to-all-start = ((bf16[4,8,2,768]{3,2,0,1:T(2,128)(2,1)}), bf16[4,8,2,768]{3,2,0,1:T(2,128)(2,1)S(1)}, u32[]{:S(2)}, u32[]{:S(2)}) async-start(bf16[4,8,2,768]{3,2,0,1:T(2,128)(2,1)} %copy.32), calls=%async_computation | async-start | bytes 196608 | tf_op jit(solution)/shard_map/all_to_all | solution.py:49
  19.3 0.7 fusion.65
  20.1 1.6 %convolution_convert_fusion.2 = bf16[4,16,768]{2,1,0:T(8,128)(2,1)S(1)} fusion(bf16[4,196,768]{2,0,1:T(4,128)(2,1)} %param.6, f32[4,16]{1,0:T(4,128)S(1)} %get-tuple-element.18, f32[4,196,16]{1,2,0:T(8,128)S(1)} %fusion.32), kind=kOutput, calls=%fused_computation.18 | convolution fusion | flops 19354628 | bytes 1352960 | tf_op jit(solution)/shard_map/bms,bmd->bsd/dot_general | solution.py:39
  21.7 0.7 copy.35
  22.4 4.0 %all-to-all-done = bf16[4,8,2,768]{3,2,0,1:T(2,128)(2,1)S(1)} async-done(((bf16[4,8,2,768]{3,2,0,1:T(2,128)(2,1)}), bf16[4,8,2,768]{3,2,0,1:T(2,128)(2,1)S(1)}, u32[]{:S(2)}, u32[]{:S(2)}) %all-to-all-start) | async-done | bytes 98336 | tf_op jit(solution)/shard_map/all_to_all | solution.py:49
  26.5 3.4 %all-to-all-start.1 = ((bf16[4,8,2,768]{3,2,0,1:T(2,128)(2,1)}), bf16[4,8,2,768]{3,2,0,1:T(2,128)(2,1)S(1)}, u32[]{:S(2)}, u32[]{:S(2)}) async-start(bf16[4,8,2,768]{3,2,0,1:T(2,128)(2,1)} %copy.35), calls=%async_computation.1 | async-start | bytes 196608 | tf_op jit(solution)/shard_map/all_to_all | solution.py:48
  29.8 0.0 reduce-scatter.6.cloned.1.call-start
  29.9 1.9 %all_gather.6 = bf16[64,1,2,768]{3,2,1,0:T(2,128)(2,1)S(1)} all-gather(bf16[32,1,2,768]{3,2,1,0:T(2,128)(2,1)S(1)} %bitcast.73), channel_id=1, replica_groups=mesh['expert'=8,'pair'=2,'dp'=2] {'pair'}, dimensions={0}, use_global_device_ids=true | all-gather | bytes 294912 | tf_op jit(solution)/shard_map/all_gather | solution.py:53
  31.8 0.1 reshape_squeeze.6
  31.9 5.0 %all-to-all-done.1 = bf16[4,8,2,768]{3,2,0,1:T(2,128)(2,1)S(1)} async-done(((bf16[4,8,2,768]{3,2,0,1:T(2,128)(2,1)}), bf16[4,8,2,768]{3,2,0,1:T(2,128)(2,1)S(1)}, u32[]{:S(2)}, u32[]{:S(2)}) %all-to-all-start.1) | async-done | bytes 98336 | tf_op jit(solution)/shard_map/all_to_all | solution.py:48
  36.9 1.9 %all_gather.7 = bf16[64,1,2,768]{3,2,1,0:T(2,128)(2,1)S(1)} all-gather(bf16[32,1,2,768]{3,2,1,0:T(2,128)(2,1)S(1)} %bitcast.74), channel_id=1, replica_groups=mesh['expert'=8,'pair'=2,'dp'=2] {'pair'}, dimensions={0}, use_global_device_ids=true | all-gather | bytes 294912 | tf_op jit(solution)/shard_map/all_gather | solution.py:52
  38.8 0.1 reshape_squeeze.7
  38.9 0.5 fusion.8
  39.4 1.2 copy-done.7
  40.6 1.8 %fusion.40 = bf16[128,1536]{1,0:T(8,128)(2,1)} fusion(f32[128,1536]{1,0:T(8,128)S(1)} %fusion.8, bf16[128,768]{1,0:T(8,128)(2,1)S(1)} %reshape_squeeze.6, bf16[1,1536,768]{2,1,0:T(8,128)(2,1)S(1)} %copy-done.7), kind=kOutput, calls=%fused_computation.49 | convolution fusion | flops 305922048 | bytes 3735552 | tf_op jit(solution)/shard_map/dot_general | solution.py:11
  42.4 1.9 %reshape.35 = bf16[64,2,1536]{2,1,0:T(2,128)(2,1)} reshape(bf16[128,1536]{1,0:T(8,128)(2,1)} %fusion.40) | data formatting | bytes 786432 | tf_op jit(solution)/shard_map/reshape.16
  44.3 2.6 %fusion.12 = f32[64,1,2,768]{3,0,2,1:T(8,128)} fusion(bf16[1,768,1536]{2,1,0:T(8,128)(2,1)S(1)} %copy-done, bf16[64,2,1536]{2,1,0:T(2,128)(2,1)} %reshape.35), kind=kOutput, calls=%fused_computation.17 | convolution fusion | flops 301989888 | bytes 3145728 | tf_op jit(solution)/shard_map/dot_general | solution.py:21
  46.9 0.0 reduce-scatter.6.cloned.1.call-update
  46.9 0.0 reduce-scatter.10.cloned.1.call-start
  47.0 2.3 %fusion.5 = bf16[1,1536,768]{2,1,0:T(8,128)(2,1)} fusion(bf16[128,768]{1,0:T(8,128)(2,1)S(1)} %reshape_squeeze.6, f32[128,1536]{1,0:T(8,128)S(1)} %fusion.8), kind=kOutput, calls=%fused_computation.7 | convolution fusion | flops 304939008 | bytes 3342336 | tf_op jit(solution)/shard_map/dot_general | solution.py:15
  49.3 12.2 %copy.44 = bf16[1,1536,768]{1,0,2:T(2,128)(2,1)} copy(bf16[1,1536,768]{2,1,0:T(8,128)(2,1)} %fusion.5) | data formatting | bytes 4718592
  61.5 4.4 %copy.63 = bf16[768,1,1536]{2,0,1:T(8,128)(2,1)} copy(bf16[768,1,1536]{2,1,0:T(2,128)(2,1)} %bitcast.69) | data formatting | bytes 4718592
  65.8 0.0 reduce-scatter.10.cloned.1.call-update
  65.9 0.0 reduce-scatter.8.cloned.1.call-start
  65.9 0.9 copy-done.1
  66.8 2.2 %fusion.4 = bf16[1,768,1536]{2,1,0:T(8,128)(2,1)} fusion(bf16[128,768]{1,0:T(8,128)(2,1)S(1)} %reshape_squeeze.7, bf16[128,1536]{1,0:T(8,128)(2,1)S(1)} %copy-done.1), kind=kOutput, calls=%fused_computation.6 | convolution fusion | flops 303169536 | bytes 2949120 | tf_op jit(solution)/shard_map/dot_general | solution.py:18
  69.1 0.0 reduce-scatter.8.cloned.1.call-update
  69.1 0.9 copy-done.8
  70.0 1.8 %fusion.25 = f32[4,196,16]{1,2,0:T(8,128)S(1)} fusion(bf16[4,16,768]{2,1,0:T(8,128)(2,1)S(1)} %copy-done.8, bf16[4,196,768]{2,0,1:T(4,128)(2,1)} %param.11), kind=kOutput, calls=%fused_computation.34 | convolution fusion | flops 19267584 | bytes 1352704 | tf_op jit(solution)/shard_map/bmd,bsd->bms/dot_general | solution.py:73
  71.8 1.0 convert_element_type.44
  72.8 0.7 copy.38
  73.5 3.5 %all-to-all-start.2 = ((bf16[32,1,2,768]{3,2,1,0:T(2,128)(2,1)}), bf16[32,1,2,768]{3,2,1,0:T(2,128)(2,1)S(1)}, u32[]{:S(2)}, u32[]{:S(2)}) async-start(bf16[32,1,2,768]{3,2,1,0:T(2,128)(2,1)} %copy.38), calls=%async_computation.3 | async-start | bytes 196608 | tf_op jit(solution)/shard_map/all_to_all | solution.py:70
  77.1 0.2 fusion.23
  77.3 6.8 %all-to-all-done.2 = bf16[32,1,2,768]{3,2,1,0:T(2,128)(2,1)S(1)} async-done(((bf16[32,1,2,768]{3,2,1,0:T(2,128)(2,1)}), bf16[32,1,2,768]{3,2,1,0:T(2,128)(2,1)S(1)}, u32[]{:S(2)}, u32[]{:S(2)}) %all-to-all-start.2) | async-done | bytes 98336 | tf_op jit(solution)/shard_map/all_to_all | solution.py:70
  84.1 0.1 copy.64
  84.3 1.7 %convolution_bitcast_fusion = f32[4,196,16]{1,2,0:T(8,128)S(1)} fusion(bf16[4,16,768]{2,1,0:T(8,128)(2,1)S(1)} %reshape.36, bf16[4,196,768]{2,0,1:T(4,128)(2,1)} %param.6), kind=kOutput, calls=%fused_computation.24 | convolution fusion | flops 19267584 | bytes 1352704 | tf_op jit(solution)/shard_map/bmd,bsd->bms/dot_general | solution.py:72
  85.9 0.0 copy-start.3
  86.0 2.2 %fusion.28 = f32[4,196,768]{2,1,0:T(8,128)} fusion(f32[4,196,16]{1,2,0:T(8,128)S(1)} %fusion.23, f32[4,196,16]{1,2,0:T(8,128)S(1)} %convolution_bitcast_fusion, bf16[768,16]{0,1:T(8,128)(2,1)S(1)} %copy-done.6, f32[4,196,16]{1,2,0:T(8,128)S(1)} %copy-done.4, f32[4,16]{1,0:T(4,128)S(1)} %get-tuple-element.18), kind=kOutput, calls=%fused_computation.37 | convolution fusion | flops 19355652 | bytes 2583808 | tf_op jit(solution)/shard_map/bms,ds->bmd/dot_general | solution.py:83
  88.1 3.6 %add_convert_fusion = bf16[4,196,768]{2,1,0:T(8,128)(2,1)} fusion(f32[4,196,768]{2,1,0:T(8,128)} %fusion.28, bf16[4,16,768]{2,1,0:T(8,128)(2,1)S(1)} %reshape.36, f32[4,16]{1,0:T(4,128)S(1)} %get-tuple-element.18, f32[4,196,16]{1,2,0:T(8,128)S(1)} %copy-done.3), kind=kOutput, calls=%fused_computation.8 | convolution fusion | flops 20509700 | bytes 3761408 | tf_op jit(solution)/shard_map/bms,bsd->bmd/dot_general | solution.py:81
  91.7 2.8 %copy.43 = bf16[4,196,768]{2,0,1:T(4,128)(2,1)} copy(bf16[4,196,768]{2,1,0:T(8,128)(2,1)} %add_convert_fusion) | data formatting | bytes 2408448
  94.6 1.7 %convolution_bitcast_fusion.1 = f32[768,16]{0,1:T(8,128)S(1)} fusion(f32[4,196,16]{1,2,0:T(8,128)S(1)} %fusion.23, f32[4,196,16]{1,2,0:T(8,128)S(1)} %convolution_bitcast_fusion, bf16[4,196,768]{2,0,1:T(4,128)(2,1)} %param.6, f32[4,196,16]{1,2,0:T(8,128)S(1)} %copy-done.4, f32[4,16]{1,0:T(4,128)S(1)} %get-tuple-element.18), kind=kOutput, calls=%fused_computation.33 | convolution fusion | flops 19355652 | bytes 1404160 | tf_op jit(solution)/shard_map/bmd,bms->ds/dot_general | solution.py:85
  96.3 39.8 %psum.7 = f32[768,16]{0,1:T(8,128)} all-reduce(f32[768,16]{0,1:T(8,128)S(1)} %convolution_bitcast_fusion.1), channel_id=1, replica_groups=mesh['expert'=8,'pair'=2,'dp'=2] {'expert','pair','dp'}, use_global_device_ids=true, to_apply=%region_7.0 | all-reduce | flops 12288 | bytes 98304 | tf_op jit(solution)/shard_map/psum | solution.py:86
  136.1 3.9 %reshape_bitcast_fusion = bf16[1,1536,384]{1,0,2:T(2,128)(2,1)} fusion(bf16[384,1536]{1,0:T(8,128)(2,1)} %reduce-scatter.10.cloned.1.call-done), kind=kLoop, calls=%fused_computation.10 | loop fusion | bytes 2359296
  140.1 6.4 %copy.45 = bf16[1,1536,384]{2,1,0:T(8,128)(2,1)} copy(bf16[1,1536,384]{1,0,2:T(2,128)(2,1)} %reshape_bitcast_fusion) | data formatting | bytes 2359296
  (20 shorter events, 0.2 us)
Async XLA Ops:
  7.2 31.8 %copy-start = (bf16[1,768,1536]{2,1,0:T(8,128)(2,1)S(1)}, bf16[1,768,1536]{2,1,0:T(8,128)(2,1)}, u32[]{:S(2)}) copy-start(bf16[1,768,1536]{2,1,0:T(8,128)(2,1)} %param.8) | copy-start | bytes 7077892
  9.0 12.7 %copy-start.2 = (f32[4,196,16]{1,2,0:T(8,128)}, f32[4,196,16]{1,2,0:T(8,128)S(1)}, u32[]{:S(2)}) copy-start(f32[4,196,16]{1,2,0:T(8,128)S(1)} %fusion.32) | copy-start | bytes 150532
  12.1 14.4 %all-to-all-start = ((bf16[4,8,2,768]{3,2,0,1:T(2,128)(2,1)}), bf16[4,8,2,768]{3,2,0,1:T(2,128)(2,1)S(1)}, u32[]{:S(2)}, u32[]{:S(2)}) async-start(bf16[4,8,2,768]{3,2,0,1:T(2,128)(2,1)} %copy.32), calls=%async_computation | async-start | bytes 196608 | tf_op jit(solution)/shard_map/all_to_all | solution.py:49
  26.5 10.4 %all-to-all-start.1 = ((bf16[4,8,2,768]{3,2,0,1:T(2,128)(2,1)}), bf16[4,8,2,768]{3,2,0,1:T(2,128)(2,1)S(1)}, u32[]{:S(2)}, u32[]{:S(2)}) async-start(bf16[4,8,2,768]{3,2,0,1:T(2,128)(2,1)} %copy.35), calls=%async_computation.1 | async-start | bytes 196608 | tf_op jit(solution)/shard_map/all_to_all | solution.py:48
  29.8 42.0 %reduce-scatter.6.cloned.1.call-start = ((), (), s32[]{:S(2)}) async-start(), calls=%async_computation.6 | async-start | bytes 589824 | tf_op jit(solution)/shard_map/reduce_scatter | solution.py:62
  38.9 1.7 %copy-start.7 = (bf16[1,1536,768]{2,1,0:T(8,128)(2,1)S(1)}, bf16[1,1536,768]{2,1,0:T(8,128)(2,1)}, u32[]{:S(2)}) copy-start(bf16[1,1536,768]{2,1,0:T(8,128)(2,1)} %param.9) | copy-start | bytes 7077892
  46.9 89.2 %reduce-scatter.10.cloned.1.call-start = ((), (), s32[]{:S(2)}) async-start(), calls=%async_computation.8 | async-start | bytes 3538944
  65.8 1.0 copy-start.1
  65.9 80.6 %reduce-scatter.8.cloned.1.call-start = ((), (), s32[]{:S(2)}) async-start(), calls=%async_computation.7 | async-start | bytes 3538944 | tf_op jit(solution)/shard_map/reduce_scatter | solution.py:63
  69.1 0.9 copy-start.8
  70.0 7.1 %copy-start.5 = (f32[4,196,16]{1,2,0:T(8,128)S(1)}, f32[4,196,16]{1,2,0:T(8,128)}, u32[]{:S(2)}) copy-start(f32[4,196,16]{1,2,0:T(8,128)} %get-tuple-element.17) | copy-start | bytes 150532
  73.5 12.4 %copy-start.4 = (f32[4,196,16]{1,2,0:T(8,128)S(1)}, f32[4,196,16]{1,2,0:T(8,128)}, u32[]{:S(2)}) copy-start(f32[4,196,16]{1,2,0:T(8,128)} %get-tuple-element.19) | copy-start | bytes 150532
  73.5 12.4 %copy-start.6 = (bf16[768,16]{0,1:T(8,128)(2,1)S(1)}, bf16[768,16]{0,1:T(8,128)(2,1)}, u32[]{:S(2)}) copy-start(bf16[768,16]{0,1:T(8,128)(2,1)} %param.7) | copy-start | bytes 73732
  73.5 10.6 %all-to-all-start.2 = ((bf16[32,1,2,768]{3,2,1,0:T(2,128)(2,1)}), bf16[32,1,2,768]{3,2,1,0:T(2,128)(2,1)S(1)}, u32[]{:S(2)}, u32[]{:S(2)}) async-start(bf16[32,1,2,768]{3,2,1,0:T(2,128)(2,1)} %copy.38), calls=%async_computation.3 | async-start | bytes 196608 | tf_op jit(solution)/shard_map/all_to_all | solution.py:70
  85.9 2.2 %copy-start.3 = (f32[4,196,16]{1,2,0:T(8,128)S(1)}, f32[4,196,16]{1,2,0:T(8,128)}, u32[]{:S(2)}) copy-start(f32[4,196,16]{1,2,0:T(8,128)} %copy-done.2) | copy-start | bytes 150532
Sparse Core Ops, SparseCore 0:
  47.1 5.4 reduce-scatter.5
  66.0 32.4 reduce-scatter.9
  101.3 35.5 reduce-scatter.7
where the time goes:
time: 154 us; the launch traced here: 153 us
  blocking collectives  43.7 us (28%)
  local copies, waits for them, and re-layouts  37.2 us (24%)
  matrix products  25.5 us (17%)
  waiting for transfers between devices  15.9 us (10%)
  starting transfers between devices  14.3 us (9%)
  between operations  13.9 us (9%)
  other arithmetic  2.6 us (2%)
    psum x1, blocking collectives, local(): phi_grad = lax.psum(phi_part, ('expert', 'pair', 'dp'))  39.8 us
    unnamed x23, local copies, waits for them, and re-layouts  32.8 us
    all_to_all x1, starting transfers between devices, local(): lax.all_to_all(outgoing_grad, 'expert', split_axis=1, concat_axis=0, tile...  7.28 us
    all_to_all x1, waiting for transfers between devices, local(): lax.all_to_all(back_low, 'expert', split_axis=0, concat_axis=1, tiled=True)  6.84 us
    all_to_all x1, waiting for transfers between devices, local(): lax.all_to_all(outgoing_in, 'expert', split_axis=1, concat_axis=0, tiled=...  4.98 us
    all_to_all x1, waiting for transfers between devices, local(): lax.all_to_all(outgoing_grad, 'expert', split_axis=1, concat_axis=0, tile...  4.02 us
    dot_general x1, matrix products, local(): jnp.einsum('bms,bsd->bmd', dispatch_low, slot_in_grad, preferred_element_...  3.6 us
    all_to_all x1, starting transfers between devices, local(): lax.all_to_all(back_low, 'expert', split_axis=0, concat_axis=1, tiled=True)  3.49 us
  transfers between devices with their start and end apart: 6, of which 3 were waited for; matrix products, arithmetic and copies ran while one was open for 33% of the time, Pallas kernels for 0%

commit v1 on v0

--- a/solution.py
+++ b/solution.py
@@ -2,6 +2,7 @@
 import jax.numpy as jnp
 from jax import lax
 from jax.sharding import PartitionSpec as P
+from jax.lax import all_gather
 
 
 def expert_rows(z_rows, g_rows, w_first, w_second):
@@ -83,7 +84,7 @@
         token_part + jnp.einsum("bms,ds->bmd", logit_low, phi, preferred_element_type=f32)
     ).astype(jnp.bfloat16)
     phi_part = jnp.einsum("bmd,bms->ds", tokens, logit_low, preferred_element_type=f32)
-    phi_grad = lax.psum(phi_part, ("expert", "pair", "dp"))
+    phi_grad = jnp.sum(all_gather(phi_part, axis_name=("expert", "pair", "dp")), axis=0)
     return (token_grad, phi_grad, grad_w_in, grad_w_out)
 
 

time: 154 us -> 171 us (1.11)
  waiting for transfers between devices: 15.9 us -> 62.5 us
  blocking collectives: 43.7 us -> 3.88 us
  matrix products: 25.5 us -> 27.9 us
  starting transfers between devices: 14.3 us -> 16.5 us
  other arithmetic: 2.6 us -> 4.67 us
    psum x1 -> x0, blocking collectives: 39.8 us -> none  [local(): phi_grad = lax.psum(phi_part, ('expert', 'pair', 'dp'))]
    all_gather x0 -> x1, waiting for transfers between devices: none -> 30.5 us  [local(): all_gather(phi_part, axis_name=('expert', 'pair', 'dp'))]
    reduce_scatter x1, waiting for transfers between devices: 0.01 us -> 14.2 us  [local(): lax.psum_scatter(jnp.stack(firsts).astype(jnp.bfloat16), 'dp', scatter_di...]
    reduce_scatter x1, waiting for transfers between devices: 0.01 us -> 3.23 us  [local(): back_sum = lax.psum_scatter(backs, 'pair', scatter_dimension=0, tiled=True)]
    all_to_all x1, starting transfers between devices: 3.49 us -> 5.72 us  [local(): lax.all_to_all(back_low, 'expert', split_axis=0, concat_axis=1, tiled=True)]
    unnamed x23 -> x28, local copies, waits for them, and re-layouts: 32.8 us -> 34.5 us
  transfers between devices with their start and end apart: 6 -> 7, of which waited for: 3 -> 6; matrix products, arithmetic and copies ran while one was open for 33% -> 30% of each run, Pallas kernels for 0% -> 0%
where the time goes in v1:
time: 171 us; the launch traced here: 170 us
  waiting for transfers between devices  62.5 us (37%)
  local copies, waits for them, and re-layouts  38.9 us (23%)
  matrix products  27.9 us (16%)
  starting transfers between devices  16.5 us (10%)
  between operations  15.6 us (9%)
  other arithmetic  4.67 us (3%)
  blocking collectives  3.88 us (2%)
    unnamed x28, local copies, waits for them, and re-layouts  34.5 us
    all_gather x1, waiting for transfers between devices, local(): all_gather(phi_part, axis_name=('expert', 'pair', 'dp'))  30.5 us
    reduce_scatter x1, waiting for transfers between devices, local(): lax.psum_scatter(jnp.stack(firsts).astype(jnp.bfloat16), 'dp', scatter_di...  14.2 us
    all_to_all x1, starting transfers between devices, local(): lax.all_to_all(outgoing_grad, 'expert', split_axis=1, concat_axis=0, tile...  7.28 us
    all_to_all x1, starting transfers between devices, local(): lax.all_to_all(back_low, 'expert', split_axis=0, concat_axis=1, tiled=True)  5.72 us
    all_to_all x1, waiting for transfers between devices, local(): lax.all_to_all(back_low, 'expert', split_axis=0, concat_axis=1, tiled=True)  5.49 us
    all_to_all x1, waiting for transfers between devices, local(): lax.all_to_all(outgoing_in, 'expert', split_axis=1, concat_axis=0, tiled=...  4.97 us
    all_to_all x1, waiting for transfers between devices, local(): lax.all_to_all(outgoing_grad, 'expert', split_axis=1, concat_axis=0, tile...  4.03 us
  transfers between devices with their start and end apart: 7, of which 6 were waited for; matrix products, arithmetic and copies ran while one was open for 30% of the time, Pallas kernels for 0%

profile of v1, /device:TPU:0, one launch (start us, length us, event | category | flops | bytes accessed | tf_op | source)
XLA Modules:
  0.0 170.0 jit_solution(16575623760961690871)
XLA Ops:
  8.0 1.8 %fusion.32 = f32[4,196,16]{1,2,0:T(8,128)S(1)} fusion(bf16[4,196,768]{2,0,1:T(4,128)(2,1)} %param.6, bf16[768,16]{0,1:T(8,128)(2,1)} %param.7), kind=kOutput, calls=%fused_computation.42 | convolution fusion | flops 19267584 | bytes 1278976 | tf_op jit(solution)/shard_map/bmd,ds->bms/dot_general | solution.py:35
  9.9 0.7 fusion.64
  10.5 1.6 convolution_convert_fusion.3
  12.2 0.7 copy.32
  12.9 7.3 %all-to-all-start = ((bf16[4,8,2,768]{3,2,0,1:T(2,128)(2,1)}), bf16[4,8,2,768]{3,2,0,1:T(2,128)(2,1)S(1)}, u32[]{:S(2)}, u32[]{:S(2)}) async-start(bf16[4,8,2,768]{3,2,0,1:T(2,128)(2,1)} %copy.32), calls=%async_computation | async-start | bytes 196608 | tf_op jit(solution)/shard_map/all_to_all | solution.py:50
  20.2 0.7 fusion.65
  20.9 1.6 convolution_convert_fusion.2
  22.6 0.7 copy.35
  23.3 4.0 %all-to-all-done = bf16[4,8,2,768]{3,2,0,1:T(2,128)(2,1)S(1)} async-done(((bf16[4,8,2,768]{3,2,0,1:T(2,128)(2,1)}), bf16[4,8,2,768]{3,2,0,1:T(2,128)(2,1)S(1)}, u32[]{:S(2)}, u32[]{:S(2)}) %all-to-all-start) | async-done | bytes 98336 | tf_op jit(solution)/shard_map/all_to_all | solution.py:50
  27.3 3.4 %all-to-all-start.1 = ((bf16[4,8,2,768]{3,2,0,1:T(2,128)(2,1)}), bf16[4,8,2,768]{3,2,0,1:T(2,128)(2,1)S(1)}, u32[]{:S(2)}, u32[]{:S(2)}) async-start(bf16[4,8,2,768]{3,2,0,1:T(2,128)(2,1)} %copy.35), calls=%async_computation.1 | async-start | bytes 196608 | tf_op jit(solution)/shard_map/all_to_all | solution.py:49
  30.7 1.9 %all_gather.12 = bf16[64,1,2,768]{3,2,1,0:T(2,128)(2,1)S(1)} all-gather(bf16[32,1,2,768]{3,2,1,0:T(2,128)(2,1)S(1)} %bitcast.79), channel_id=1, replica_groups=mesh['expert'=8,'pair'=2,'dp'=2] {'pair'}, dimensions={0}, use_global_device_ids=true | all-gather | bytes 294912 | tf_op jit(solution)/shard_map/all_gather | solution.py:54
  32.7 0.1 reshape_squeeze.6
  32.8 5.0 %all-to-all-done.1 = bf16[4,8,2,768]{3,2,0,1:T(2,128)(2,1)S(1)} async-done(((bf16[4,8,2,768]{3,2,0,1:T(2,128)(2,1)}), bf16[4,8,2,768]{3,2,0,1:T(2,128)(2,1)S(1)}, u32[]{:S(2)}, u32[]{:S(2)}) %all-to-all-start.1) | async-done | bytes 98336 | tf_op jit(solution)/shard_map/all_to_all | solution.py:49
  37.7 1.9 %all_gather.13 = bf16[64,1,2,768]{3,2,1,0:T(2,128)(2,1)S(1)} all-gather(bf16[32,1,2,768]{3,2,1,0:T(2,128)(2,1)S(1)} %bitcast.80), channel_id=1, replica_groups=mesh['expert'=8,'pair'=2,'dp'=2] {'pair'}, dimensions={0}, use_global_device_ids=true | all-gather | bytes 294912 | tf_op jit(solution)/shard_map/all_gather | solution.py:53
  39.7 0.1 reshape_squeeze.7
  39.8 0.5 fusion.8
  40.3 1.2 copy-done.9
  41.4 1.8 %fusion.40 = bf16[128,1536]{1,0:T(8,128)(2,1)} fusion(f32[128,1536]{1,0:T(8,128)S(1)} %fusion.8, bf16[128,768]{1,0:T(8,128)(2,1)S(1)} %reshape_squeeze.6, bf16[1,1536,768]{2,1,0:T(8,128)(2,1)S(1)} %copy-done.9), kind=kOutput, calls=%fused_computation.50 | convolution fusion | flops 305922048 | bytes 3735552 | tf_op jit(solution)/shard_map/dot_general | solution.py:12
  43.2 1.9 %reshape.35 = bf16[64,2,1536]{2,1,0:T(2,128)(2,1)} reshape(bf16[128,1536]{1,0:T(8,128)(2,1)} %fusion.40) | data formatting | bytes 786432 | tf_op jit(solution)/shard_map/reshape.16
  45.1 2.7 %fusion.12 = f32[64,1,2,768]{3,0,2,1:T(8,128)} fusion(bf16[1,768,1536]{2,1,0:T(8,128)(2,1)S(1)} %copy-done, bf16[64,2,1536]{2,1,0:T(2,128)(2,1)} %reshape.35), kind=kOutput, calls=%fused_computation.18 | convolution fusion | flops 301989888 | bytes 3145728 | tf_op jit(solution)/shard_map/dot_general | solution.py:22
  47.8 2.4 %fusion.25 = f32[4,196,16]{1,2,0:T(8,128)} fusion(bf16[4,16,768]{2,1,0:T(8,128)(2,1)S(1)} %copy-done.10, bf16[4,196,768]{2,0,1:T(4,128)(2,1)} %param.11), kind=kOutput, calls=%fused_computation.35 | convolution fusion | flops 19267584 | bytes 1352704 | tf_op jit(solution)/shard_map/bmd,bsd->bms/dot_general | solution.py:74
  50.2 3.2 %reduce-scatter.6.cloned.1.call-done = f32[32,1,2,768]{3,0,2,1:T(8,128)} async-done(((f32[64,1,2,768]{3,0,2,1:T(8,128)}), f32[32,1,2,768]{3,0,2,1:T(8,128)}) %reduce-scatter.6.cloned.1.call-update) | async-done | bytes 196624 | tf_op jit(solution)/shard_map/reduce_scatter | solution.py:63
  53.4 0.9 convert_element_type.44
  54.4 0.7 copy.38
  55.1 5.7 %all-to-all-start.2 = ((bf16[32,1,2,768]{3,2,1,0:T(2,128)(2,1)}), bf16[32,1,2,768]{3,2,1,0:T(2,128)(2,1)S(1)}, u32[]{:S(2)}, u32[]{:S(2)}) async-start(bf16[32,1,2,768]{3,2,1,0:T(2,128)(2,1)} %copy.38), calls=%async_computation.3 | async-start | bytes 196608 | tf_op jit(solution)/shard_map/all_to_all | solution.py:71
  60.9 1.6 fusion.23
  62.4 5.5 %all-to-all-done.2 = bf16[32,1,2,768]{3,2,1,0:T(2,128)(2,1)S(1)} async-done(((bf16[32,1,2,768]{3,2,1,0:T(2,128)(2,1)}), bf16[32,1,2,768]{3,2,1,0:T(2,128)(2,1)S(1)}, u32[]{:S(2)}, u32[]{:S(2)}) %all-to-all-start.2) | async-done | bytes 98336 | tf_op jit(solution)/shard_map/all_to_all | solution.py:71
  67.9 0.1 copy.65
  68.1 1.7 convolution_bitcast_fusion
  69.7 2.5 %convolution_bitcast_fusion.1 = f32[768,16]{0,1:T(8,128)} fusion(f32[4,196,16]{1,2,0:T(8,128)} %fusion.23, f32[4,196,16]{1,2,0:T(8,128)S(1)} %convolution_bitcast_fusion, bf16[4,196,768]{2,0,1:T(4,128)(2,1)} %param.6, f32[4,196,16]{1,2,0:T(8,128)} %get-tuple-element.19, f32[4,16]{1,0:T(4,128)S(1)} %get-tuple-element.18), kind=kOutput, calls=%fused_computation.34 | convolution fusion | flops 19355652 | bytes 1404160 | tf_op jit(solution)/shard_map/bmd,bms->ds/dot_general | solution.py:86
  72.3 0.0 reduce-scatter.10.cloned.1.call-start
  72.4 3.3 %fusion.5 = bf16[1,1536,768]{2,1,0:T(8,128)(2,1)} fusion(bf16[128,768]{1,0:T(8,128)(2,1)} %copy-done.2, f32[128,1536]{1,0:T(8,128)S(1)} %fusion.8), kind=kOutput, calls=%fused_computation.7 | convolution fusion | flops 304939008 | bytes 3342336 | tf_op jit(solution)/shard_map/dot_general | solution.py:16
  75.6 12.2 %copy.44 = bf16[1,1536,768]{1,0,2:T(2,128)(2,1)} copy(bf16[1,1536,768]{2,1,0:T(8,128)(2,1)} %fusion.5) | data formatting | bytes 4718592
  87.8 4.4 %copy.64 = bf16[768,1,1536]{2,0,1:T(8,128)(2,1)} copy(bf16[768,1,1536]{2,1,0:T(2,128)(2,1)} %bitcast.74) | data formatting | bytes 4718592
  92.2 0.0 reduce-scatter.8.cloned.1.call-start
  92.2 0.9 copy-done.1
  93.1 2.2 %fusion.4 = bf16[1,768,1536]{2,1,0:T(8,128)(2,1)} fusion(bf16[128,768]{1,0:T(8,128)(2,1)S(1)} %reshape_squeeze.7, bf16[128,1536]{1,0:T(8,128)(2,1)S(1)} %copy-done.1), kind=kOutput, calls=%fused_computation.6 | convolution fusion | flops 303169536 | bytes 2949120 | tf_op jit(solution)/shard_map/dot_general | solution.py:19
  95.4 0.8 copy-done.5
  96.2 0.1 copy-done.6
  96.3 2.2 %fusion.28 = f32[4,196,768]{2,1,0:T(8,128)} fusion(f32[4,196,16]{1,2,0:T(8,128)S(1)} %copy-done.6, f32[4,196,16]{1,2,0:T(8,128)S(1)} %convolution_bitcast_fusion, bf16[768,16]{0,1:T(8,128)(2,1)S(1)} %copy-done.8, f32[4,196,16]{1,2,0:T(8,128)S(1)} %copy-done.5, f32[4,16]{1,0:T(4,128)S(1)} %get-tuple-element.18), kind=kOutput, calls=%fused_computation.38 | convolution fusion | flops 19355652 | bytes 2583808 | tf_op jit(solution)/shard_map/bms,ds->bmd/dot_general | solution.py:84
  98.4 3.7 %add_convert_fusion = bf16[4,196,768]{2,1,0:T(8,128)(2,1)} fusion(f32[4,196,768]{2,1,0:T(8,128)} %fusion.28, bf16[4,16,768]{2,1,0:T(8,128)(2,1)S(1)} %reshape.36, f32[4,16]{1,0:T(4,128)S(1)} %get-tuple-element.18, f32[4,196,16]{1,2,0:T(8,128)S(1)} %copy-done.4), kind=kOutput, calls=%fused_computation.8 | convolution fusion | flops 20509700 | bytes 3761408 | tf_op jit(solution)/shard_map/bms,bsd->bmd/dot_general | solution.py:82
  102.1 2.8 %copy.43 = bf16[4,196,768]{2,0,1:T(4,128)(2,1)} copy(bf16[4,196,768]{2,1,0:T(8,128)(2,1)} %add_convert_fusion) | data formatting | bytes 2408448
  104.9 30.5 %all-gather.3.cloned.1.call-done = f32[24576,16]{0,1:T(8,128)} async-done(((f32[768,16]{0,1:T(8,128)}), f32[24576,16]{0,1:T(8,128)}) %all-gather.3.cloned.1.call-update) | async-done | bytes 1572880 | tf_op jit(solution)/shard_map/all_gather | solution.py:87
  135.4 1.9 %copy.47 = f32[2,8,32,768]{3,2,1,0:T(8,128)S(1)} copy(f32[2,8,32,768]{3,1,2,0:T(8,128)} %bitcast.76) | data formatting | bytes 3145728
  137.3 0.8 bitcast_reduce_fusion
  138.0 3.9 %reshape_bitcast_fusion = bf16[1,1536,384]{1,0,2:T(2,128)(2,1)} fusion(bf16[384,1536]{1,0:T(8,128)(2,1)} %reduce-scatter.10.cloned.1.call-done), kind=kLoop, calls=%fused_computation.10 | loop fusion | bytes 2359296
  141.9 6.4 %copy.45 = bf16[1,1536,384]{2,1,0:T(8,128)(2,1)} copy(bf16[1,1536,384]{1,0,2:T(2,128)(2,1)} %reshape_bitcast_fusion) | data formatting | bytes 2359296
  148.4 14.2 %reduce-scatter.8.cloned.1.call-done = bf16[1,384,1536]{2,1,0:T(8,128)(2,1)} async-done(((bf16[1,768,1536]{2,1,0:T(8,128)(2,1)}), bf16[1,384,1536]{2,1,0:T(8,128)(2,1)}) %reduce-scatter.8.cloned.1.call-update) | async-done | bytes 1179664 | tf_op jit(solution)/shard_map/reduce_scatter | solution.py:64
  (28 shorter events, 0.3 us)
Async XLA Ops:
  8.0 31.7 %copy-start = (bf16[1,768,1536]{2,1,0:T(8,128)(2,1)S(1)}, bf16[1,768,1536]{2,1,0:T(8,128)(2,1)}, u32[]{:S(2)}) copy-start(bf16[1,768,1536]{2,1,0:T(8,128)(2,1)} %param.8) | copy-start | bytes 7077892
  9.9 12.7 %copy-start.3 = (f32[4,196,16]{1,2,0:T(8,128)}, f32[4,196,16]{1,2,0:T(8,128)S(1)}, u32[]{:S(2)}) copy-start(f32[4,196,16]{1,2,0:T(8,128)S(1)} %fusion.32) | copy-start | bytes 150532
  12.9 14.4 %all-to-all-start = ((bf16[4,8,2,768]{3,2,0,1:T(2,128)(2,1)}), bf16[4,8,2,768]{3,2,0,1:T(2,128)(2,1)S(1)}, u32[]{:S(2)}, u32[]{:S(2)}) async-start(bf16[4,8,2,768]{3,2,0,1:T(2,128)(2,1)} %copy.32), calls=%async_computation | async-start | bytes 196608 | tf_op jit(solution)/shard_map/all_to_all | solution.py:50
  27.3 10.4 %all-to-all-start.1 = ((bf16[4,8,2,768]{3,2,0,1:T(2,128)(2,1)}), bf16[4,8,2,768]{3,2,0,1:T(2,128)(2,1)S(1)}, u32[]{:S(2)}, u32[]{:S(2)}) async-start(bf16[4,8,2,768]{3,2,0,1:T(2,128)(2,1)} %copy.35), calls=%async_computation.1 | async-start | bytes 196608 | tf_op jit(solution)/shard_map/all_to_all | solution.py:49
  30.7 22.7 %reduce-scatter.6.cloned.1.call-start = ((), (), s32[]{:S(2)}) async-start(), calls=%async_computation.6 | async-start | bytes 589824 | tf_op jit(solution)/shard_map/reduce_scatter | solution.py:63
  32.7 7.5 %copy-start.2 = (bf16[128,768]{1,0:T(8,128)(2,1)}, bf16[128,768]{1,0:T(8,128)(2,1)S(1)}, u32[]{:S(2)}) copy-start(bf16[128,768]{1,0:T(8,128)(2,1)S(1)} %reshape_squeeze.6) | copy-start | bytes 589828
  39.7 1.7 copy-start.9
  45.1 2.7 %copy-start.10 = (bf16[4,16,768]{2,1,0:T(8,128)(2,1)S(1)}, bf16[4,16,768]{2,1,0:T(8,128)(2,1)}, u32[]{:S(2)}) copy-start(bf16[4,16,768]{2,1,0:T(8,128)(2,1)} %param.10) | copy-start | bytes 294916
  47.8 13.1 %copy-start.7 = (f32[4,196,16]{1,2,0:T(8,128)S(1)}, f32[4,196,16]{1,2,0:T(8,128)}, u32[]{:S(2)}) copy-start(f32[4,196,16]{1,2,0:T(8,128)} %get-tuple-element.17) | copy-start | bytes 150532
  55.1 12.8 %all-to-all-start.2 = ((bf16[32,1,2,768]{3,2,1,0:T(2,128)(2,1)}), bf16[32,1,2,768]{3,2,1,0:T(2,128)(2,1)S(1)}, u32[]{:S(2)}, u32[]{:S(2)}) async-start(bf16[32,1,2,768]{3,2,1,0:T(2,128)(2,1)} %copy.38), calls=%async_computation.3 | async-start | bytes 196608 | tf_op jit(solution)/shard_map/all_to_all | solution.py:71
  60.8 74.6 %all-gather.3.cloned.1.call-start = ((), (), s32[]{:S(2)}) async-start(), calls=%async_computation.8 | async-start | bytes 1622016 | tf_op jit(solution)/shard_map/all_gather | solution.py:87
  72.3 65.7 %reduce-scatter.10.cloned.1.call-start = ((), (), s32[]{:S(2)}) async-start(), calls=%async_computation.9 | async-start | bytes 3538944
  92.1 1.0 copy-start.1
  92.2 70.4 %reduce-scatter.8.cloned.1.call-start = ((), (), s32[]{:S(2)}) async-start(), calls=%async_computation.7 | async-start | bytes 3538944 | tf_op jit(solution)/shard_map/reduce_scatter | solution.py:64
  95.4 0.9 copy-start.5
  95.4 0.9 copy-start.6
  95.4 0.9 copy-start.8
  96.3 2.2 %copy-start.4 = (f32[4,196,16]{1,2,0:T(8,128)S(1)}, f32[4,196,16]{1,2,0:T(8,128)}, u32[]{:S(2)}) copy-start(f32[4,196,16]{1,2,0:T(8,128)} %copy-done.3) | copy-start | bytes 150532
Sparse Core Ops, SparseCore 0:
  47.9 5.4 reduce-scatter.5
  72.4 62.9 all-gather.2
Sparse Core Ops, SparseCore 1:
  92.3 32.9 reduce-scatter.9
  127.8 34.7 reduce-scatter.7
